TPU v7x, 256 devices: a whole 4x4x8 slice. The times are simulated.
256 devices in a mesh: ctx: 64 (over x, z, core), head: 4 (over y).
Axes of the slice: x: 4, y: 4, z: 8, core: 2. Of those that a mesh axis runs over, the one named last changes fastest.
Arguments:
- x_stream: bfloat16 [16384, 4096], P('ctx', 'head'), may hold values from -6 to 6
- z_stream: bfloat16 [16384, 4096], P('ctx', 'head'), may hold values from -6 to 6
- b_stream: bfloat16 [16384, 512], P('ctx', 'head'), may hold values from -6 to 6
- c_stream: bfloat16 [16384, 512], P('ctx', 'head'), may hold values from -6 to 6
- step_size: float32 [16384, 64], P('ctx', 'head'), may hold values from 0 to 3
- log_decay: float32 [16384, 64], P('ctx', 'head'), may hold values from -1 to 0
- kernel_x: bfloat16 [4, 4096], P(None, 'head'), may hold values from -3 to 3
- kernel_b: bfloat16 [4, 512], P(None, 'head'), may hold values from -3 to 3
- kernel_c: bfloat16 [4, 512], P(None, 'head'), may hold values from -3 to 3
- skip_gain: float32 [64], P('head'), may hold values from 1 to 8
- norm_gain: float32 [4096], P('head'), may hold values from 0.25 to 1.75
- out_weight: bfloat16 [4096, 4096], P('head'), may hold values from -0.125 to 0.125
Outputs:
- layer_out: bfloat16 [16384, 4096], P('ctx', 'head')
All inputs are finite; a program needn't handle non-finite values.
Results may differ from a plain program's by a relative error of at most 0.013.
Values may be sent and summed in bfloat16 or wider, within the bound.
A program may use at most 128 MiB of HBM per device.

v0:
```python
import jax
import jax.numpy as jnp
from jax import lax
from jax.sharding import PartitionSpec as P

P_SIZE = 64
N = 128
CONV = 4
SPAN = 256


def passed_along(x, axis, by):
    length = lax.axis_size(axis)
    pairs = [(i, i + by) for i in range(length) if 0 <= i + by < length]
    return lax.ppermute(x, axis, pairs)


def carried_in(x, axis, join, neutral):
    place = lax.axis_index(axis)
    gathered = jax.tree.map(
        lambda a, kind: lax.all_gather(a.astype(kind), axis), x, (jnp.bfloat16, jnp.bfloat16)
    )
    state = jax.tree.map(lambda a, e: jnp.zeros_like(a) + jnp.asarray(e, a.dtype), x, neutral)

    def one(step, state):
        return join(
            state,
            jax.tree.map(
                lambda a, own: lax.dynamic_index_in_dim(a, step, 0, False).astype(own.dtype),
                gathered,
                x,
            ),
        )

    return lax.fori_loop(0, place, one, state)


def conv_rimmed(rimmed, kernel, length):
    running = jnp.zeros((length, rimmed.shape[1]), jnp.float32)
    for offset in range(CONV):
        running = running + rimmed[offset : offset + length].astype(jnp.float32) * kernel[
            offset
        ].astype(jnp.float32)
    return jax.nn.silu(running).astype(jnp.bfloat16)


def span_step(carry_state, pieces):
    x_block, b_block, c_block, step_block, decay_block = pieces
    cumlog = jnp.cumsum(decay_block, axis=0)
    scores = jnp.einsum("tgn,sgn->gts", c_block, b_block, preferred_element_type=jnp.float32)
    decay_sums = jnp.transpose(cumlog, (1, 2, 0))
    decay_gap = decay_sums[:, :, :, None] - decay_sums[:, :, None, :]
    causal = jnp.arange(SPAN)[:, None] >= jnp.arange(SPAN)[None, :]
    factor_ts = jnp.where(causal, jnp.exp(jnp.where(causal, decay_gap, 0.0)), 0.0)
    step_cols = jnp.transpose(step_block, (1, 2, 0))[:, :, None, :]
    mixing = (scores[:, None] * factor_ts * step_cols).astype(jnp.bfloat16)
    intra_out = jnp.einsum("gkts,sgkp->tgkp", mixing, x_block, preferred_element_type=jnp.float32)
    carried = (
        jnp.einsum(
            "tgn,gkpn->tgkp",
            c_block.astype(jnp.float32),
            carry_state,
            precision=lax.Precision.HIGHEST,
        )
        * jnp.exp(cumlog)[..., None]
    )
    block_total = cumlog[-1]
    input_weight = jnp.exp(block_total[None] - cumlog) * step_block
    scaled = (x_block.astype(jnp.float32) * input_weight[..., None]).astype(jnp.bfloat16)
    new_state = jnp.exp(block_total)[..., None, None] * carry_state + jnp.einsum(
        "tgkp,tgn->gkpn", scaled, b_block, preferred_element_type=jnp.float32
    )
    return (new_state, intra_out + carried)


def combine_heads(earlier, later_part):
    return (
        earlier[0] + later_part[0],
        jnp.exp(later_part[0])[:, None, None] * earlier[1] + later_part[1],
    )


def body(
    x_stream,
    z_stream,
    b_stream,
    c_stream,
    step_size,
    log_decay,
    kernel_x,
    kernel_b,
    kernel_c,
    skip_gain,
    norm_gain,
    out_weight,
):
    margin = CONV - 1
    rim_x, rim_b, rim_c = passed_along(
        (x_stream[-margin:], b_stream[-margin:], c_stream[-margin:]), "ctx", 1
    )
    length = x_stream.shape[0]
    x_conv = conv_rimmed(jnp.concatenate([rim_x, x_stream], axis=0), kernel_x, length)
    b_conv = conv_rimmed(jnp.concatenate([rim_b, b_stream], axis=0), kernel_b, length)
    c_conv = conv_rimmed(jnp.concatenate([rim_c, c_stream], axis=0), kernel_c, length)
    head_count = step_size.shape[1]
    group_count = b_stream.shape[1] // N
    per_group = head_count // group_count
    span_count = length // SPAN
    x_spans = x_conv.reshape(span_count, SPAN, group_count, per_group, P_SIZE)
    b_spans = b_conv.reshape(span_count, SPAN, group_count, N)
    c_spans = c_conv.reshape(span_count, SPAN, group_count, N)
    step_spans = step_size.reshape(span_count, SPAN, group_count, per_group)
    decay_spans = log_decay.reshape(span_count, SPAN, group_count, per_group)
    zero_state = jnp.zeros((group_count, per_group, P_SIZE, N), jnp.float32)
    final_state, ssd_local = lax.scan(
        span_step, zero_state, (x_spans, b_spans, c_spans, step_spans, decay_spans)
    )
    ssd_local = ssd_local.reshape(length, group_count, per_group, P_SIZE)
    totals = jnp.sum(log_decay, axis=0)
    final_flat = final_state.reshape(head_count, P_SIZE, N)
    prefix = carried_in(
        (totals, final_flat),
        "ctx",
        combine_heads,
        (jnp.zeros_like(totals), jnp.zeros_like(final_flat)),
    )
    incoming = prefix[1]
    cumlog_all = jnp.cumsum(log_decay, axis=0)
    c_float = c_conv.astype(jnp.float32).reshape(length, group_count, N)
    correction = jnp.einsum(
        "tgn,gkpn->tgkp",
        c_float,
        incoming.reshape(group_count, per_group, P_SIZE, N),
        precision=lax.Precision.HIGHEST,
    ) * jnp.exp(cumlog_all).reshape(length, group_count, per_group, 1)
    ssd_out = (ssd_local + correction).reshape(length, head_count, P_SIZE)
    ssd_out = ssd_out + skip_gain[None, :, None] * x_conv.astype(jnp.float32).reshape(
        length, head_count, P_SIZE
    )
    channels = head_count * P_SIZE
    gated_out = ssd_out.reshape(length, channels) * jax.nn.silu(z_stream.astype(jnp.float32))
    grouped = gated_out.reshape(length, group_count, per_group * P_SIZE)
    inverse_rms = lax.rsqrt(jnp.mean(grouped * grouped, axis=2, keepdims=True) + 1e-05)
    normed = ((grouped * inverse_rms).reshape(length, channels) * norm_gain[None, :]).astype(
        jnp.bfloat16
    )
    partial_out = jnp.dot(normed, out_weight, preferred_element_type=jnp.float32)
    summed = lax.psum_scatter(
        partial_out.astype(jnp.bfloat16), "head", scatter_dimension=1, tiled=True
    )
    return summed


def solution(mesh):
    placed = (
        P("ctx", "head"),
        P("ctx", "head"),
        P("ctx", "head"),
        P("ctx", "head"),
        P("ctx", "head"),
        P("ctx", "head"),
        P(None, "head"),
        P(None, "head"),
        P(None, "head"),
        P("head"),
        P("head"),
        P("head", None),
    )
    return jax.shard_map(
        body, mesh=mesh, in_specs=placed, out_specs=P("ctx", "head"), check_vma=False
    )
```

profile of v0, /device:TPU:4, one launch (start us, length us, event | category | flops | bytes accessed | tf_op | source)
XLA Modules:
  0.0 273.6 jit_solution(4322339555626133662)
XLA Ops:
  6.6 0.8 slice.88
  7.4 0.2 copy.30
  7.6 1.9 collective-permute-start
  9.5 0.7 slice.104
  10.2 3.9 %collective-permute-start.2 = (bf16[3,128]{1,0:T(4,128)(2,1)S(1)}, bf16[3,128]{1,0:T(4,128)(2,1)S(1)}, u32[]{:S(2)}, u32[]{:S(2)}) collective-permute-start(bf16[3,128]{1,0:T(4,128)(2,1)S(1)} %slice.104), channel_id=1, source_target_pairs={{0,4},{4,8},{8,12},{12,16},{16,20},{20,24},{24,28},{28,32},{32,36}... | collective-permute-start | bytes 2312 | tf_op jit(solution)/shard_map/ppermute | solution.py:15
  14.1 0.7 copy_bitcast_fusion.1
  14.9 0.6 reduce-window.14
  15.4 0.2 slice_reduce_fusion.1
  15.9 0.3 slice_reduce_fusion.2
  16.1 0.9 slice_convert_fusion.3
  17.0 0.8 bitcast_convert_fusion.3
  17.8 0.8 reshape_bitcast_fusion
  18.7 1.2 copy.31
  19.9 1.1 multiply_convert_fusion.7
  21.1 1.5 fusion.13
  22.5 1.0 fusion.12
  23.6 1.9 collective-permute-start.1
  25.6 0.1 reduce_sum.18
  25.7 0.2 copy.39
  25.9 0.6 reduce-window.16
  26.5 0.2 slice_reduce_fusion
  26.7 0.6 dynamic-slice
  27.9 0.2 dynamic-update-slice
  28.1 110.8 %all-reduce = bf16[1024]{0:T(1024)(128)(2,1)S(1)} all-reduce(bf16[1024]{0:T(1024)(128)(2,1)S(1)} %dynamic-update-slice), channel_id=2, replica_groups=mesh['ctx'=64,'head'=4] {'ctx'}, use_global_device_ids=true, to_apply=%add | all-reduce | flops 1024 | bytes 4096
  139.4 0.2 fusion.35
  139.6 1.4 fusion.7
  141.1 37.1 %while.3 = (s32[]{:T(128)}, f32[16,64,128]{2,1,0:T(8,128)S(1)}, s32[]{:T(128)}, bf16[64,16]{1,0:T(8,128)(2,1)S(1)}, bf16[64,16,64,128]{3,2,1,0:T(8,128)(2,1)}, /*index=5*/s32[]{:T(128)}, s32[]{:T(128)}, s32[]{:T(128)}) while((s32[]{:T(128)}, f32[16,64,128]{2,1,0:T(8,128)S(1)}, s32[]{:T(128)}, bf16[64,16]{1,0:T(8,128)(2,1)S(1)}, ...), condition=%wide.region_4.5_spmd, body=%wide.region_3.4_spmd.sunk | while | flops 393237 | bytes 1311015 | solution.py:35
  141.1 1.1 convert_add_fusion.2
  142.3 1.1 convert_add_fusion.2
  143.4 1.1 convert_add_fusion.2
  144.6 1.1 convert_add_fusion.2
  145.7 1.1 convert_add_fusion.2
  146.9 1.1 convert_add_fusion.2
  148.0 1.1 convert_add_fusion.2
  149.2 1.1 convert_add_fusion.2
  150.4 1.1 convert_add_fusion.2
  151.5 1.1 convert_add_fusion.2
  152.7 1.1 convert_add_fusion.2
  153.8 1.1 convert_add_fusion.2
  155.0 1.1 convert_add_fusion.2
  156.2 1.1 convert_add_fusion.2
  157.3 1.1 convert_add_fusion.2
  158.5 1.1 convert_add_fusion.2
  159.6 1.1 convert_add_fusion.2
  160.8 1.1 convert_add_fusion.2
  161.9 1.1 convert_add_fusion.2
  163.1 1.1 convert_add_fusion.2
  164.3 1.1 convert_add_fusion.2
  165.4 1.1 convert_add_fusion.2
  166.6 1.1 convert_add_fusion.2
  167.7 1.1 convert_add_fusion.2
  168.9 1.1 convert_add_fusion.2
  170.0 1.1 convert_add_fusion.2
  171.2 1.1 convert_add_fusion.2
  172.4 1.1 convert_add_fusion.2
  173.5 1.1 convert_add_fusion.2
  174.7 1.1 convert_add_fusion.2
  175.8 1.1 convert_add_fusion.2
  177.0 1.1 convert_add_fusion.2
  178.1 0.6 fusion.11
  178.7 0.6 fusion.10
  179.4 0.5 multiply_reduce_fusion
  179.8 7.2 %convolution_convert_fusion = bf16[256,4096]{1,0:T(8,128)(2,1)} fusion(bf16[1024,4096]{1,0:T(8,128)(2,1)} %param.25, f32[256,1024]{0,1:T(8,128)S(1)} %get-tuple-element.85, f32[1024]{0:T(1024)S(1)} %copy-done.3, f32[256]{0:T(256)S(1)} %add_rsqrt_fusion), kind=kOutput, calls=%fused_computation.2 | convolution fusion | flops 2149318656 | bytes 11539456 | tf_op jit(solution)/shard_map/dot_general | solution.py:147
  187.1 79.7 %reduce-scatter.2.cloned.1.call-done = bf16[256,1024]{1,0:T(8,128)(2,1)} async-done(((bf16[256,4096]{1,0:T(8,128)(2,1)}), bf16[256,1024]{1,0:T(8,128)(2,1)}) %reduce-scatter.2.cloned.1.call-update) | async-done | bytes 524304 | tf_op jit(solution)/shard_map/reduce_scatter | solution.py:148
  (80 shorter events, 1.5 us)
Async XLA Ops:
  6.5 20.2 %copy-start.6 = (u32[256]{0:T(256)S(1)}, u32[256]{0:T(256)}, u32[]{:S(2)}) copy-start(u32[256]{0:T(256)} %constant.65) | copy-start | bytes 3076
  6.5 19.0 %copy-start.1 = (f32[256,16]{0,1:T(8,128)S(1)}, f32[256,16]{0,1:T(8,128)}, u32[]{:S(2)}) copy-start(f32[256,16]{0,1:T(8,128)} %param.19) | copy-start | bytes 49156
  6.5 17.1 %copy-start.2 = (bf16[256,128]{1,0:T(8,128)(2,1)S(1)}, bf16[256,128]{1,0:T(8,128)(2,1)}, u32[]{:S(2)}) copy-start(bf16[256,128]{1,0:T(8,128)(2,1)} %param.17) | copy-start | bytes 196612
  6.5 19.2 %copy-start = (bf16[256,1024]{1,0:T(8,128)(2,1)S(1)}, bf16[256,1024]{1,0:T(8,128)(2,1)}, u32[]{:S(2)}) copy-start(bf16[256,1024]{1,0:T(8,128)(2,1)} %param.15) | copy-start | bytes 1572868
  6.5 132.4 %copy-start.4 = (bf16[4,128]{1,0:T(4,128)(2,1)S(1)}, bf16[4,128]{1,0:T(4,128)(2,1)}, u32[]{:S(2)}) copy-start(bf16[4,128]{1,0:T(4,128)(2,1)} %param.22) | copy-start | bytes 3076
  6.5 132.5 %copy-start.5 = (f32[16]{0:T(128)S(1)}, f32[16]{0:T(128)}, u32[]{:S(2)}) copy-start(f32[16]{0:T(128)} %param.23) | copy-start | bytes 196
  6.6 134.4 %all-gather.4.cloned.1.call-start = ((), (), s32[]{:S(2)}) async-start(), calls=%async_computation.2 | async-start | bytes 17039360 | tf_op jit(solution)/shard_map/all_gather | solution.py:21
  7.6 13.5 %collective-permute-start = (bf16[3,1024]{0,1:T(8,128)(2,1)S(1)}, bf16[3,1024]{0,1:T(8,128)(2,1)S(1)}, u32[]{:S(2)}, u32[]{:S(2)}) collective-permute-start(bf16[3,1024]{0,1:T(8,128)(2,1)S(1)} %copy.30), channel_id=1, source_target_pairs={{0,4},{4,8},{8,12},{12,16},{16,20},{20,24},{24,28},{28,32},{32,36}... | collective-permute-start | bytes 18440 | tf_op jit(solution)/shard_map/ppermute | solution.py:15
  10.2 9.7 %collective-permute-start.2 = (bf16[3,128]{1,0:T(4,128)(2,1)S(1)}, bf16[3,128]{1,0:T(4,128)(2,1)S(1)}, u32[]{:S(2)}, u32[]{:S(2)}) collective-permute-start(bf16[3,128]{1,0:T(4,128)(2,1)S(1)} %slice.104), channel_id=1, source_target_pairs={{0,4},{4,8},{8,12},{12,16},{16,20},{20,24},{24,28},{28,32},{32,36}... | collective-permute-start | bytes 2312 | tf_op jit(solution)/shard_map/ppermute | solution.py:15
  23.6 243.2 %reduce-scatter.2.cloned.1.call-start = ((), (), s32[]{:S(2)}) async-start(), calls=%async_computation.1 | async-start | bytes 2621440 | tf_op jit(solution)/shard_map/reduce_scatter | solution.py:148
  23.6 115.7 %collective-permute-start.1 = (bf16[3,128]{1,0:T(4,128)(2,1)S(1)}, bf16[3,128]{1,0:T(4,128)(2,1)S(1)}, u32[]{:S(2)}, u32[]{:S(2)}) collective-permute-start(bf16[3,128]{1,0:T(4,128)(2,1)S(1)} %slice.96), channel_id=1, source_target_pairs={{0,4},{4,8},{8,12},{12,16},{16,20},{20,24},{24,28},{28,32},{32,36}... | collective-permute-start | bytes 2312 | tf_op jit(solution)/shard_map/ppermute | solution.py:15
  178.1 1.7 copy-start.3
Sparse Core Ops, SparseCore 0:
  23.7 100.2 all-gather.3
  187.2 79.5 reduce-scatter.1
where the time goes:
time: 277 us; the launch traced here: 274 us
  blocking collectives  111 us (40%)
  waiting for transfers between devices  79.7 us (29%)
  other arithmetic  43.2 us (16%)
  between operations  14.3 us (5%)
  matrix products  11 us (4%)
  starting transfers between devices  7.84 us (3%)
  local copies, waits for them, and re-layouts  5.77 us (2%)
    unnamed x1, blocking collectives  111 us
    reduce_scatter x1, waiting for transfers between devices, body(): lax.psum_scatter(partial_out.astype(jnp.bfloat16), 'head', scatter_dimens...  79.7 us
    add x32, other arithmetic, combine_heads(): jnp.exp(later_part[0])[:, None, None] * earlier[1] + later_part[1]  35.6 us
    ppermute x3, starting transfers between devices, passed_along(): return lax.ppermute(x, axis, pairs)  7.76 us
    dot_general x1, matrix products, body(): jnp.dot(normed, out_weight, preferred_element_type=jnp.float32)  7.2 us
  transfers between devices with their start and end apart: 5, of which 1 were waited for; matrix products, arithmetic and copies ran while one was open for 4% of the time, Pallas kernels for 0%

commit v1 on v0

v1 whole, which is shorter than its diff:
```python
import jax
import jax.numpy as jnp
from jax import lax
from jax.experimental import pallas as pl
from jax.experimental.pallas import tpu as pltpu
from jax.sharding import PartitionSpec as P

TOK = 256
CH = 1024
HEADS = 16
N = 128
LINE = 16
XS = 4
ROWS = N // LINE
PIECES = 4
PW = CH // PIECES
MESH = pl.DeviceIdType.MESH
F32 = jnp.float32
BF16 = jnp.bfloat16


def dot(a, b):
    return jnp.dot(a, b, preferred_element_type=F32)


def split3(v):
    hi = v.astype(BF16)
    rest = v - hi.astype(F32)
    mid = rest.astype(BF16)
    low = (rest - mid.astype(F32)).astype(BF16)
    return hi, mid, low


def dot_exact_right(v, onehot):
    hi, mid, low = split3(v)
    return dot(hi, onehot) + dot(mid, onehot) + dot(low, onehot)


def dot_exact_left(onehot, v):
    hi, mid, low = split3(v)
    return dot(onehot, hi) + dot(onehot, mid) + dot(onehot, low)


def silu(v):
    return v * (1.0 / (1.0 + jnp.exp(-v)))


def spread(rows, lanes, width):
    head = lax.broadcasted_iota(jnp.int32, (rows, lanes), 0)
    lane = lax.broadcasted_iota(jnp.int32, (rows, lanes), 1)
    return ((lane >= head * width) & (lane < head * width + width)).astype(F32).astype(BF16)


def conv_rolled(v, k):
    total = k[3:4] * v
    for shift in (1, 2, 3):
        total = total + k[3 - shift : 4 - shift] * pltpu.roll(v, shift, 0)
    return silu(total)


def conv_head(halo, v, k):
    joined = jnp.concatenate([halo[8:16].astype(F32), v[0:16].astype(F32)], axis=0)
    return conv_rolled(joined, k)[8:24]


def kernel(
    x_hbm, z_hbm, b_ref, c_ref, step_ref, decay_ref, kx_ref, kb_ref, kc_ref, skip_ref, gain_ref,
    w_hbm, o_ref,
    x_v, z_v, w_v, xc, bc, cc, halo_x, halo_b, halo_c,
    cum_t, step_t, cum_wide, in_w, gate_a, gate_b, scores, skip_wide,
    dl_send, dl_recv, dlx_send, dlx_recv,
    st_send, st_recv, excl, g_send, g_recv, pf_send, pf_recv, normed,
    diag_send, diag_recv, near_send, near_keep, near_recv, own,
    local_sem, halo_ssem, halo_rsem, dl_ssem, dl_rsem, dlx_ssem, dlx_rsem,
    st_ssem, st_rsem, g_ssem, g_rsem, pf_ssem, pf_rsem,
    diag_ssem, diag_rsem, near_ssem, near_rsem,
):
    ctx = lax.axis_index("ctx")
    y = lax.axis_index("head")
    ctx_count = LINE * XS
    xi = ctx // LINE
    pos = lax.rem(ctx, LINE)
    base = xi * LINE
    right = lax.rem(y + 1, 4)
    left = lax.rem(y + 3, 4)
    across = lax.rem(y + 2, 4)

    barrier = pltpu.get_barrier_semaphore()

    def greet_line(i, carry):
        pl.semaphore_signal(
            barrier, inc=1, device_id={"ctx": base + lax.rem(pos + i, LINE)}, device_id_type=MESH
        )
        return carry

    def greet_x(i, carry):
        pl.semaphore_signal(
            barrier, inc=1, device_id={"ctx": lax.rem(xi + i, XS) * LINE + pos}, device_id_type=MESH
        )
        return carry

    lax.fori_loop(1, LINE, greet_line, 0)
    lax.fori_loop(1, XS, greet_x, 0)
    for near in (right, left):
        pl.semaphore_signal(barrier, inc=1, device_id={"head": near}, device_id_type=MESH)
    for step in (1, ctx_count - 1):
        pl.semaphore_signal(
            barrier, inc=1, device_id={"ctx": lax.rem(ctx + step, ctx_count)}, device_id_type=MESH
        )

    load_x = pltpu.make_async_copy(x_hbm, x_v, local_sem.at[0])
    load_z = pltpu.make_async_copy(z_hbm, z_v, local_sem.at[1])
    load_w = pltpu.make_async_copy(w_hbm, w_v, local_sem.at[2])
    load_x.start()
    load_z.start()
    load_w.start()

    row = lax.broadcasted_iota(jnp.int32, (TOK, TOK), 0)
    col = lax.broadcasted_iota(jnp.int32, (TOK, TOK), 1)
    lower = (row >= col).astype(F32).astype(BF16)
    step = step_ref[...]
    cum = dot_exact_left(lower, decay_ref[...])
    last = cum[TOK - 1 : TOK, :]
    weight = jnp.exp(last - cum) * step
    cum_t[...] = cum.T
    step_t[...] = step.T
    wide = spread(HEADS, HEADS * 128, 128)
    expand = spread(HEADS, CH, 64)
    cum_wide[...] = dot_exact_right(cum, wide)
    in_w[...] = dot_exact_right(weight, expand)
    dl_send[...] = dot_exact_right(jnp.broadcast_to(last, (8, HEADS)), spread(HEADS, N, 1))[0:1]

    load_x.wait()

    def conv_block(p, carry):
        lanes = pl.ds(pl.multiple_of(p * 128, 128), 128)
        xc[:, lanes] = conv_rolled(x_v[:, lanes].astype(F32), kx_ref[:, lanes].astype(F32)).astype(BF16)
        return carry

    lax.fori_loop(0, CH // 128, conv_block, 0)
    bc[...] = conv_rolled(b_ref[...].astype(F32), kb_ref[...].astype(F32)).astype(BF16)
    cc[...] = conv_rolled(c_ref[...].astype(F32), kc_ref[...].astype(F32)).astype(BF16)

    pl.semaphore_wait(barrier, LINE - 1 + XS - 1 + 2 + 2)

    def halo_copies():
        parts = ((x_v, halo_x), (b_ref, halo_b), (c_ref, halo_c))
        return [
            pltpu.make_async_remote_copy(
                src_ref=src.at[pl.ds(TOK - 16, 16)],
                dst_ref=dst,
                send_sem=halo_ssem.at[i],
                recv_sem=halo_rsem.at[i],
                device_id={"ctx": lax.rem(ctx + 1, ctx_count)},
                device_id_type=MESH,
            )
            for i, (src, dst) in enumerate(parts)
        ]

    for copy in halo_copies():
        copy.start()

    def dl_copy(i, slot):
        to = lax.rem(pos + i, LINE)
        return pltpu.make_async_remote_copy(
            src_ref=dl_send,
            dst_ref=dl_recv.at[slot],
            send_sem=dl_ssem.at[i],
            recv_sem=dl_rsem.at[slot],
            device_id={"ctx": base + to},
            device_id_type=MESH,
        )

    def st_copy(i, slot):
        to = lax.rem(pos + i, LINE)
        return pltpu.make_async_remote_copy(
            src_ref=st_send.at[to],
            dst_ref=st_recv.at[slot],
            send_sem=st_ssem.at[i],
            recv_sem=st_rsem.at[slot],
            device_id={"ctx": base + to},
            device_id_type=MESH,
        )

    def pf_copy(i, slot):
        to = lax.rem(pos + i, LINE)
        return pltpu.make_async_remote_copy(
            src_ref=pf_send.at[to],
            dst_ref=pf_recv.at[slot],
            send_sem=pf_ssem.at[i],
            recv_sem=pf_rsem.at[slot],
            device_id={"ctx": base + to},
            device_id_type=MESH,
        )

    def dlx_copy(i, slot):
        return pltpu.make_async_remote_copy(
            src_ref=dlx_send,
            dst_ref=dlx_recv.at[slot],
            send_sem=dlx_ssem.at[i],
            recv_sem=dlx_rsem.at[slot],
            device_id={"ctx": lax.rem(xi + i, XS) * LINE + pos},
            device_id_type=MESH,
        )

    def g_copy(i, slot):
        return pltpu.make_async_remote_copy(
            src_ref=g_send,
            dst_ref=g_recv.at[slot],
            send_sem=g_ssem.at[i],
            recv_sem=g_rsem.at[slot],
            device_id={"ctx": lax.rem(xi + i, XS) * LINE + pos},
            device_id_type=MESH,
        )

    def start_all(make, count, here):
        def one(i, carry):
            make(i, here).start()
            return carry

        lax.fori_loop(1, count, one, 0)

    def wait_all(make, count, here):
        def one(i, carry):
            copy = make(i, lax.rem(here + i, count))
            copy.wait_send()
            copy.wait_recv()
            return carry

        lax.fori_loop(1, count, one, 0)

    start_all(dl_copy, LINE, pos)

    for copy in halo_copies():
        copy.wait()

    first = ctx == 0

    def halo_value(ref):
        v = ref[...].astype(F32)
        return jnp.where(first, jnp.zeros_like(v), v)

    xc[0:16, :] = conv_head(halo_value(halo_x), x_v[0:16, :], kx_ref[...].astype(F32)).astype(BF16)
    bc[0:16, :] = conv_head(halo_value(halo_b), b_ref[0:16, :], kb_ref[...].astype(F32)).astype(BF16)
    cc[0:16, :] = conv_head(halo_value(halo_c), c_ref[0:16, :], kc_ref[...].astype(F32)).astype(BF16)

    b_cols = bc[...].astype(F32).T.astype(BF16)

    def state_block(p, carry):
        lanes = pl.ds(pl.multiple_of(p * 128, 128), 128)
        scaled = (xc[:, lanes].astype(F32) * in_w[:, lanes]).astype(BF16)
        st_send[:, :, lanes] = dot(b_cols, scaled).reshape(LINE, ROWS, 128).astype(BF16)
        return carry

    lax.fori_loop(0, CH // 128, state_block, 0)
    st_recv[pos] = st_send[pos]
    start_all(st_copy, LINE, pos)

    dl_recv[pos] = dl_send[...]
    wait_all(dl_copy, LINE, pos)
    line_decay = dl_recv[:, 0, :]
    dlx_send[...] = jnp.sum(line_decay, axis=0, keepdims=True)
    dlx_recv[xi] = dlx_send[...]
    start_all(dlx_copy, XS, xi)

    scores[...] = dot(cc[...], b_cols)
    in_w[...] = dot_exact_right(jnp.exp(cum), expand)
    skip_row = dot_exact_right(jnp.broadcast_to(skip_ref[...], (8, HEADS)), expand)[0:1]
    skip_wide[...] = skip_row
    load_z.wait()
    trow = lax.broadcasted_iota(jnp.int32, (128, 128), 0)
    tcol = lax.broadcasted_iota(jnp.int32, (128, 128), 1)
    causal = trow >= tcol

    def span_block(p, carry):
        lanes = pl.ds(pl.multiple_of(p * 128, 128), 128)
        x_pair = xc[:, lanes]
        tops, bottoms = [], []
        for e in range(2):
            h = 2 * p + e
            cols = cum_wide[:, pl.ds(pl.multiple_of(h * 128, 128), 128)]
            cum_row = cum_t[pl.ds(h, 1), :]
            step_row = step_t[pl.ds(h, 1), :]

            def mix(t, s, masked):
                gap = cols[t : t + 128] - cum_row[:, s : s + 128]
                if masked:
                    gap = jnp.where(causal, gap, -1e30)
                m = scores[t : t + 128, s : s + 128] * jnp.exp(gap) * step_row[:, s : s + 128]
                return m.astype(BF16)

            tops.append(dot(mix(0, 0, True), x_pair[0:128]))
            bottoms.append(
                dot(mix(128, 0, False), x_pair[0:128]) + dot(mix(128, 128, True), x_pair[128:256])
            )
        low = tcol < 64
        inner = jnp.concatenate(
            [jnp.where(low, tops[0], tops[1]), jnp.where(low, bottoms[0], bottoms[1])], axis=0
        )
        gate = silu(z_v[:, lanes].astype(F32))
        gate_a[:, lanes] = (inner + skip_wide[:, lanes] * x_pair.astype(F32)) * gate
        gate_b[:, lanes] = in_w[:, lanes] * gate
        return carry

    lax.fori_loop(0, CH // 128, span_block, 0)

    expand_n = spread(N, CH, 64)
    line_factor = jnp.exp(dot_exact_right(line_decay, expand_n))
    wait_all(st_copy, LINE, pos)
    running = jnp.zeros((ROWS, CH), F32)
    for j in range(LINE):
        excl[j] = running
        running = line_factor[j : j + 1] * running + st_recv[j].astype(F32)
    g_send[...] = running
    start_all(g_copy, XS, xi)

    wait_all(dlx_copy, XS, xi)
    x_decay = dlx_recv[:, 0, :]
    x_factor = jnp.exp(
        dot_exact_right(jnp.concatenate([x_decay, x_decay], axis=0), expand_n)
    )
    wait_all(g_copy, XS, xi)
    before = jnp.zeros((ROWS, CH), F32)
    for i in range(XS - 1):
        before = jnp.where(i < xi, x_factor[i : i + 1] * before + g_recv[i], before)
    for j in range(LINE):
        pf_send[j] = (excl[j] + before).astype(BF16)
        before = line_factor[j : j + 1] * before
    pf_recv[pos] = pf_send[pos]
    start_all(pf_copy, LINE, pos)
    wait_all(pf_copy, LINE, pos)

    state = pf_recv[...].astype(F32).reshape(N, CH).astype(BF16)
    c_all = cc[...]
    squares = jnp.zeros((TOK, 128), F32)
    for p in range(CH // 256):
        lanes = slice(p * 256, p * 256 + 256)
        gated = gate_a[:, lanes] + dot(c_all, state[:, lanes]) * gate_b[:, lanes]
        gate_a[:, lanes] = gated
        sq = gated * gated
        squares = squares + sq[:, 0:128] + sq[:, 128:256]
    scale = lax.rsqrt(jnp.sum(squares, axis=1, keepdims=True) * (1.0 / CH) + 1e-05)
    for p in range(CH // 256):
        lanes = slice(p * 256, p * 256 + 256)
        normed[:, lanes] = (gate_a[:, lanes] * scale * gain_ref[:, lanes]).astype(BF16)

    load_w.wait()

    def product(owner, j):
        lanes = pl.ds(pl.multiple_of(owner * CH + j * PW, PW), PW)
        return dot(normed[...], w_v[:, lanes])

    sides = (right, left)
    diag_rows = (0, 128)
    near_rows = (128, 0)

    def diag_copy(side, j):
        return pltpu.make_async_remote_copy(
            src_ref=diag_send.at[side, j],
            dst_ref=diag_recv.at[side, j],
            send_sem=diag_ssem.at[side, j],
            recv_sem=diag_rsem.at[side, j],
            device_id={"head": sides[side]},
            device_id_type=MESH,
        )

    def near_copy(side, relayed, j):
        return pltpu.make_async_remote_copy(
            src_ref=near_send.at[side, relayed, j],
            dst_ref=near_recv.at[side, relayed, j],
            send_sem=near_ssem.at[side, relayed, j],
            recv_sem=near_rsem.at[side, relayed, j],
            device_id={"head": sides[side]},
            device_id_type=MESH,
        )

    def across_step(j, carry):
        part = product(across, j).astype(BF16)
        for side in range(2):
            diag_send[side, j] = part[diag_rows[side] : diag_rows[side] + 128]
            diag_copy(side, j).start()
        return carry

    lax.fori_loop(0, PIECES, across_step, 0)

    def near_step(j, carry):
        for side in range(2):
            part = product(sides[side], j).astype(BF16)
            near_send[side, 0, j] = part[near_rows[side] : near_rows[side] + 128]
            near_copy(side, 0, j).start()
            near_keep[side, j] = part[diag_rows[side] : diag_rows[side] + 128]
        return carry

    lax.fori_loop(0, PIECES, near_step, 0)

    def relay_step(j, carry):
        for side in range(2):
            diag_copy(side, j).wait()
            total = near_keep[side, j].astype(F32) + diag_recv[side, j].astype(F32)
            near_send[side, 1, j] = total.astype(BF16)
            near_copy(side, 1, j).start()
        return carry

    lax.fori_loop(0, PIECES, relay_step, 0)

    def own_step(j, carry):
        own[j] = product(y, j)
        return carry

    lax.fori_loop(0, PIECES, own_step, 0)

    for relayed in range(2):
        def last_step(j, carry):
            for side in range(2):
                near_copy(side, relayed, j).wait()
            return carry

        lax.fori_loop(0, PIECES, last_step, 0)
    for j in range(PIECES):
        lanes = slice(j * PW, j * PW + PW)
        mine = own[j].astype(BF16).astype(F32)
        top = near_recv[0, 1, j].astype(F32) + near_recv[1, 0, j].astype(F32)
        bottom = near_recv[0, 0, j].astype(F32) + near_recv[1, 1, j].astype(F32)
        o_ref[0:128, lanes] = (mine[0:128] + top).astype(BF16)
        o_ref[128:256, lanes] = (mine[128:256] + bottom).astype(BF16)


def body(x, z, b, c, step, decay, kx, kb, kc, skip, gain, w):
    vm = pl.BlockSpec(memory_space=pltpu.VMEM)
    hbm = pl.BlockSpec(memory_space=pl.ANY)
    dma = pltpu.SemaphoreType.DMA
    return pl.pallas_call(
        kernel,
        out_shape=jax.ShapeDtypeStruct((TOK, CH), BF16),
        in_specs=[hbm, hbm] + [vm] * 9 + [hbm],
        out_specs=vm,
        scratch_shapes=[
            pltpu.VMEM((TOK, CH), BF16),
            pltpu.VMEM((TOK, CH), BF16),
            pltpu.VMEM((CH, 4 * CH), BF16),
            pltpu.VMEM((TOK, CH), BF16),
            pltpu.VMEM((TOK, N), BF16),
            pltpu.VMEM((TOK, N), BF16),
            pltpu.VMEM((16, CH), BF16),
            pltpu.VMEM((16, N), BF16),
            pltpu.VMEM((16, N), BF16),
            pltpu.VMEM((HEADS, TOK), F32),
            pltpu.VMEM((HEADS, TOK), F32),
            pltpu.VMEM((TOK, HEADS * 128), F32),
            pltpu.VMEM((TOK, CH), F32),
            pltpu.VMEM((TOK, CH), F32),
            pltpu.VMEM((TOK, CH), F32),
            pltpu.VMEM((TOK, TOK), F32),
            pltpu.VMEM((1, CH), F32),
            pltpu.VMEM((1, N), F32),
            pltpu.VMEM((LINE, 1, N), F32),
            pltpu.VMEM((1, N), F32),
            pltpu.VMEM((XS, 1, N), F32),
            pltpu.VMEM((LINE, ROWS, CH), BF16),
            pltpu.VMEM((LINE, ROWS, CH), BF16),
            pltpu.VMEM((LINE, ROWS, CH), F32),
            pltpu.VMEM((ROWS, CH), F32),
            pltpu.VMEM((XS, ROWS, CH), F32),
            pltpu.VMEM((LINE, ROWS, CH), BF16),
            pltpu.VMEM((LINE, ROWS, CH), BF16),
            pltpu.VMEM((TOK, CH), BF16),
            pltpu.VMEM((2, PIECES, 128, PW), BF16),
            pltpu.VMEM((2, PIECES, 128, PW), BF16),
            pltpu.VMEM((2, 2, PIECES, 128, PW), BF16),
            pltpu.VMEM((2, PIECES, 128, PW), BF16),
            pltpu.VMEM((2, 2, PIECES, 128, PW), BF16),
            pltpu.VMEM((PIECES, TOK, PW), F32),
            dma((3,)),
            dma((3,)),
            dma((3,)),
            dma((LINE,)),
            dma((LINE,)),
            dma((XS,)),
            dma((XS,)),
            dma((LINE,)),
            dma((LINE,)),
            dma((XS,)),
            dma((XS,)),
            dma((LINE,)),
            dma((LINE,)),
            dma((2, PIECES)),
            dma((2, PIECES)),
            dma((2, 2, PIECES)),
            dma((2, 2, PIECES)),
        ],
        compiler_params=pltpu.CompilerParams(collective_id=0, has_side_effects=True),
        name="ssm_layer",
    )(x, z, b, c, step, decay, kx, kb, kc, skip.reshape(1, HEADS), gain.reshape(1, CH), w)


def solution(mesh):
    placed = (
        P("ctx", "head"),
        P("ctx", "head"),
        P("ctx", "head"),
        P("ctx", "head"),
        P("ctx", "head"),
        P("ctx", "head"),
        P(None, "head"),
        P(None, "head"),
        P(None, "head"),
        P("head"),
        P("head"),
        P("head", None),
    )
    return jax.shard_map(
        body, mesh=mesh, in_specs=placed, out_specs=P("ctx", "head"), check_vma=False
    )
```

time: 277 us -> 62.3 us (0.22)
  blocking collectives: 111 us -> 0 us
  waiting for transfers between devices: 79.7 us -> 0 us
  Pallas kernels: 0 us -> 56.8 us
  other arithmetic: 43.2 us -> 0 us
  between operations: 14.3 us -> 0.01 us
  matrix products: 11 us -> 0 us
  starting transfers between devices: 7.84 us -> 0 us
    unnamed x1 -> x0, blocking collectives: 111 us -> none
    reduce_scatter x1 -> x0, waiting for transfers between devices: 79.7 us -> none  [body(): lax.psum_scatter(partial_out.astype(jnp.bfloat16), 'head', scatter_dimens...]
    pallas_call x0 -> x1, Pallas kernels: none -> 56.8 us  [body(): pl.pallas_call(kernel, out_shape=jax.ShapeDtypeStruct((TOK, CH), BF16), i...]
    add x32 -> x0, other arithmetic: 35.6 us -> none  [combine_heads(): jnp.exp(later_part[0])[:, None, None] * earlier[1] + later_part[1]]
    dot_general x6 -> x0, matrix products: 11 us -> none  [the longest x1 7.2 us: body(): jnp.dot(normed, out_weight, preferred_element_type=jnp.float32)]
    ppermute x3 -> x0, starting transfers between devices: 7.76 us -> none  [passed_along(): return lax.ppermute(x, axis, pairs)]
  transfers between devices with their start and end apart: 5 -> 0, of which waited for: 1 -> 0; matrix products, arithmetic and copies ran while one was open for 4% -> 0% of each run, Pallas kernels for 0% -> 0%
where the time goes in v1:
time: 62.3 us; the launch traced here: 61.6 us
  Pallas kernels  56.8 us (91%)
  local copies, waits for them, and re-layouts  4.81 us (8%)
    pallas_call x1, Pallas kernels, body(): pl.pallas_call(kernel, out_shape=jax.ShapeDtypeStruct((TOK, CH), BF16), i...  56.8 us
    unnamed x3, local copies, waits for them, and re-layouts  4.81 us

profile of v1, /device:TPU:4, one launch (start us, length us, event | category | flops | bytes accessed | tf_op | source)
XLA Modules:
  0.0 61.6 jit_solution(15796472625505281533)
XLA Ops:
  0.0 1.5 %copy.13.step_ref = f32[256,16]{1,0:T(8,128)} copy(f32[256,16]{0,1:T(8,128)} %param.16) | data formatting | bytes 32768 | tf_op args[4]
  1.5 1.5 %copy.14.decay_ref = f32[256,16]{1,0:T(8,128)} copy(f32[256,16]{0,1:T(8,128)} %param.17) | data formatting | bytes 32768 | tf_op args[5]
  2.9 56.8 %ssm_layer.1 = bf16[256,1024]{1,0:T(8,128)(2,1)} custom-call(bf16[256,1024]{1,0:T(8,128)(2,1)} %x_hbm.1, bf16[256,1024]{1,0:T(8,128)(2,1)} %z_hbm.1, bf16[256,128]{1,0:T(8,128)(2,1)} %b_ref.1, bf16[256,128]{1,0:T(8,128)(2,1)} %c_ref.1, f32[256,16]{1,0:T(8,128)} %copy.13.step_ref, f32[256,16]{1,0:T(8,128)} %copy.14.decay_ref, bf16[4,1024]{1,0:T(4,128)(2,1)} %kx_ref.1, ...), custom_call_target="tpu_custom_call" | custom-call | tf_op jit(solution)/shard_map/ssm_layer/pallas_call | solution.py:432
  59.8 1.9 %copy.16 = bf16[256,1024]{1,0:T(8,128)(2,1)} copy(bf16[256,1024]{1,0:T(8,128)(2,1)} %ssm_layer.1) | data formatting | bytes 1048576

commit v2 on v1

--- a/solution.py
+++ b/solution.py
@@ -64,10 +64,10 @@
 
 
 def kernel(
-    x_hbm, z_hbm, b_ref, c_ref, step_ref, decay_ref, kx_ref, kb_ref, kc_ref, skip_ref, gain_ref,
+    x_hbm, z_hbm, b_ref, c_ref, step_t, decay_t, kx_ref, kb_ref, kc_ref, skip_ref, gain_ref,
     w_hbm, o_ref,
     x_v, z_v, w_v, xc, bc, cc, halo_x, halo_b, halo_c,
-    cum_t, step_t, cum_wide, in_w, gate_a, gate_b, scores, skip_wide,
+    cum_t, cum_wide, in_w, gate_a, gate_b, scores, skip_wide,
     dl_send, dl_recv, dlx_send, dlx_recv,
     st_send, st_recv, excl, g_send, g_recv, pf_send, pf_recv, normed,
     diag_send, diag_recv, near_send, near_keep, near_recv, own,
@@ -117,13 +117,12 @@
 
     row = lax.broadcasted_iota(jnp.int32, (TOK, TOK), 0)
     col = lax.broadcasted_iota(jnp.int32, (TOK, TOK), 1)
-    lower = (row >= col).astype(F32).astype(BF16)
-    step = step_ref[...]
-    cum = dot_exact_left(lower, decay_ref[...])
+    upper = (row <= col).astype(F32).astype(BF16)
+    sums = dot_exact_right(decay_t[...], upper)
+    cum_t[...] = sums
+    cum = sums.T
     last = cum[TOK - 1 : TOK, :]
-    weight = jnp.exp(last - cum) * step
-    cum_t[...] = cum.T
-    step_t[...] = step.T
+    weight = (jnp.exp(sums[:, TOK - 1 : TOK] - sums) * step_t[...]).T
     wide = spread(HEADS, HEADS * 128, 128)
     expand = spread(HEADS, CH, 64)
     cum_wide[...] = dot_exact_right(cum, wide)
@@ -213,6 +212,22 @@
             device_id_type=MESH,
         )
 
+    def start_later(make):
+        for i in range(1, XS):
+            @pl.when(xi + i < XS)
+            def _(i=i):
+                make(i, xi).start()
+
+    def wait_earlier(make):
+        for i in range(1, XS):
+            @pl.when(xi + i < XS)
+            def _(i=i):
+                make(i, xi).wait_send()
+
+            @pl.when(xi >= i)
+            def _(i=i):
+                make(i, xi - i).wait_recv()
+
     def start_all(make, count, here):
         def one(i, carry):
             make(i, here).start()
@@ -312,14 +327,14 @@
         excl[j] = running
         running = line_factor[j : j + 1] * running + st_recv[j].astype(F32)
     g_send[...] = running
-    start_all(g_copy, XS, xi)
+    start_later(g_copy)
 
     wait_all(dlx_copy, XS, xi)
     x_decay = dlx_recv[:, 0, :]
     x_factor = jnp.exp(
         dot_exact_right(jnp.concatenate([x_decay, x_decay], axis=0), expand_n)
     )
-    wait_all(g_copy, XS, xi)
+    wait_earlier(g_copy)
     before = jnp.zeros((ROWS, CH), F32)
     for i in range(XS - 1):
         before = jnp.where(i < xi, x_factor[i : i + 1] * before + g_recv[i], before)
@@ -444,7 +459,6 @@
             pltpu.VMEM((16, CH), BF16),
             pltpu.VMEM((16, N), BF16),
             pltpu.VMEM((16, N), BF16),
-            pltpu.VMEM((HEADS, TOK), F32),
             pltpu.VMEM((HEADS, TOK), F32),
             pltpu.VMEM((TOK, HEADS * 128), F32),
             pltpu.VMEM((TOK, CH), F32),
@@ -490,7 +504,7 @@
         ],
         compiler_params=pltpu.CompilerParams(collective_id=0, has_side_effects=True),
         name="ssm_layer",
-    )(x, z, b, c, step, decay, kx, kb, kc, skip.reshape(1, HEADS), gain.reshape(1, CH), w)
+    )(x, z, b, c, step.T, decay.T, kx, kb, kc, skip.reshape(1, HEADS), gain.reshape(1, CH), w)
 
 
 def solution(mesh):

time: 62.3 us -> 58.9 us (0.945)
  local copies, waits for them, and re-layouts: 4.81 us -> 1.87 us
    unnamed x3 -> x1, local copies, waits for them, and re-layouts: 4.81 us -> 1.87 us
where the time goes in v2:
time: 58.9 us; the launch traced here: 58.7 us
  Pallas kernels  56.8 us (96%)
  local copies, waits for them, and re-layouts  1.87 us (3%)
    pallas_call x1, Pallas kernels, body(): pl.pallas_call(kernel, out_shape=jax.ShapeDtypeStruct((TOK, CH), BF16), i...  56.8 us
    unnamed x1, local copies, waits for them, and re-layouts  1.87 us

profile of v2, /device:TPU:4, one launch (start us, length us, event | category | flops | bytes accessed | tf_op | source)
XLA Modules:
  0.0 58.7 jit_solution(14605443047919221884)
XLA Ops:
  0.0 56.8 %ssm_layer.1 = bf16[256,1024]{1,0:T(8,128)(2,1)} custom-call(bf16[256,1024]{1,0:T(8,128)(2,1)} %x_hbm.1, bf16[256,1024]{1,0:T(8,128)(2,1)} %z_hbm.1, bf16[256,128]{1,0:T(8,128)(2,1)} %b_ref.1, bf16[256,128]{1,0:T(8,128)(2,1)} %c_ref.1, f32[16,256]{1,0:T(8,128)} %bitcast.4, f32[16,256]{1,0:T(8,128)} %bitcast.5, bf16[4,1024]{1,0:T(4,128)(2,1)} %kx_ref.1, ...), custom_call_target="tpu_custom_call" | custom-call | tf_op jit(solution)/shard_map/ssm_layer/pallas_call | solution.py:447
  56.8 1.9 %copy.14 = bf16[256,1024]{1,0:T(8,128)(2,1)} copy(bf16[256,1024]{1,0:T(8,128)(2,1)} %ssm_layer.1) | data formatting | bytes 1048576

commit v3 on v2

--- a/solution.py
+++ b/solution.py
@@ -13,6 +13,7 @@
 XS = 4
 ROWS = N // LINE
 PIECES = 4
+EARLY = 3
 PW = CH // PIECES
 MESH = pl.DeviceIdType.MESH
 F32 = jnp.float32
@@ -136,9 +137,7 @@
         xc[:, lanes] = conv_rolled(x_v[:, lanes].astype(F32), kx_ref[:, lanes].astype(F32)).astype(BF16)
         return carry
 
-    lax.fori_loop(0, CH // 128, conv_block, 0)
-    bc[...] = conv_rolled(b_ref[...].astype(F32), kb_ref[...].astype(F32)).astype(BF16)
-    cc[...] = conv_rolled(c_ref[...].astype(F32), kc_ref[...].astype(F32)).astype(BF16)
+    lax.fori_loop(0, EARLY, conv_block, 0)
 
     pl.semaphore_wait(barrier, LINE - 1 + XS - 1 + 2 + 2)
 
@@ -245,6 +244,10 @@
         lax.fori_loop(1, count, one, 0)
 
     start_all(dl_copy, LINE, pos)
+
+    lax.fori_loop(EARLY, CH // 128, conv_block, 0)
+    bc[...] = conv_rolled(b_ref[...].astype(F32), kb_ref[...].astype(F32)).astype(BF16)
+    cc[...] = conv_rolled(c_ref[...].astype(F32), kc_ref[...].astype(F32)).astype(BF16)
 
     for copy in halo_copies():
         copy.wait()

time: 58.9 us -> 58.7 us (level)
  no operation moved by 1% of the time
where the time goes in v3:
time: 58.7 us; the launch traced here: 58.2 us
  Pallas kernels  56.3 us (96%)
  local copies, waits for them, and re-layouts  1.87 us (3%)
    pallas_call x1, Pallas kernels, body(): pl.pallas_call(kernel, out_shape=jax.ShapeDtypeStruct((TOK, CH), BF16), i...  56.3 us
    unnamed x1, local copies, waits for them, and re-layouts  1.87 us

profile of v3, /device:TPU:4, one launch (start us, length us, event | category | flops | bytes accessed | tf_op | source)
XLA Modules:
  0.0 58.2 jit_solution(11333511060992219520)
XLA Ops:
  0.0 56.3 %ssm_layer.1 = bf16[256,1024]{1,0:T(8,128)(2,1)} custom-call(bf16[256,1024]{1,0:T(8,128)(2,1)} %x_hbm.1, bf16[256,1024]{1,0:T(8,128)(2,1)} %z_hbm.1, bf16[256,128]{1,0:T(8,128)(2,1)} %b_ref.1, bf16[256,128]{1,0:T(8,128)(2,1)} %c_ref.1, f32[16,256]{1,0:T(8,128)} %bitcast.4, f32[16,256]{1,0:T(8,128)} %bitcast.5, bf16[4,1024]{1,0:T(4,128)(2,1)} %kx_ref.1, ...), custom_call_target="tpu_custom_call" | custom-call | tf_op jit(solution)/shard_map/ssm_layer/pallas_call | solution.py:450
  56.3 1.9 %copy.14 = bf16[256,1024]{1,0:T(8,128)(2,1)} copy(bf16[256,1024]{1,0:T(8,128)(2,1)} %ssm_layer.1) | data formatting | bytes 1048576

commit v4 on v2

--- a/solution.py
+++ b/solution.py
@@ -321,10 +321,16 @@
 
     expand_n = spread(N, CH, 64)
     line_factor = jnp.exp(dot_exact_right(line_decay, expand_n))
-    wait_all(st_copy, LINE, pos)
     running = jnp.zeros((ROWS, CH), F32)
     for j in range(LINE):
         excl[j] = running
+
+        @pl.when(pos != j)
+        def _(j=j):
+            copy = st_copy(lax.rem(j - pos + LINE, LINE), j)
+            copy.wait_send()
+            copy.wait_recv()
+
         running = line_factor[j : j + 1] * running + st_recv[j].astype(F32)
     g_send[...] = running
     start_later(g_copy)
@@ -335,14 +341,21 @@
         dot_exact_right(jnp.concatenate([x_decay, x_decay], axis=0), expand_n)
     )
     wait_earlier(g_copy)
+    def start_prefix(j):
+        @pl.when(pos != j)
+        def _():
+            pf_copy(lax.rem(j - pos + LINE, LINE), pos).start()
+
     before = jnp.zeros((ROWS, CH), F32)
     for i in range(XS - 1):
         before = jnp.where(i < xi, x_factor[i : i + 1] * before + g_recv[i], before)
     for j in range(LINE):
         pf_send[j] = (excl[j] + before).astype(BF16)
         before = line_factor[j : j + 1] * before
+        if j > 0:
+            start_prefix(j - 1)
     pf_recv[pos] = pf_send[pos]
-    start_all(pf_copy, LINE, pos)
+    start_prefix(LINE - 1)
     wait_all(pf_copy, LINE, pos)
 
     state = pf_recv[...].astype(F32).reshape(N, CH).astype(BF16)
@@ -424,14 +437,15 @@
 
     lax.fori_loop(0, PIECES, own_step, 0)
 
-    for relayed in range(2):
-        def last_step(j, carry):
-            for side in range(2):
-                near_copy(side, relayed, j).wait()
-            return carry
-
-        lax.fori_loop(0, PIECES, last_step, 0)
+    def first_step(j, carry):
+        for side in range(2):
+            near_copy(side, 0, j).wait()
+        return carry
+
+    lax.fori_loop(0, PIECES, first_step, 0)
     for j in range(PIECES):
+        for side in range(2):
+            near_copy(side, 1, j).wait()
         lanes = slice(j * PW, j * PW + PW)
         mine = own[j].astype(BF16).astype(F32)
         top = near_recv[0, 1, j].astype(F32) + near_recv[1, 0, j].astype(F32)

time: 58.9 us -> 57 us (0.968)
  Pallas kernels: 56.8 us -> 54.7 us
    pallas_call x1, Pallas kernels: 56.8 us -> 54.7 us  [body(): pl.pallas_call(kernel, out_shape=jax.ShapeDtypeStruct((TOK, CH), BF16), i...]
where the time goes in v4:
time: 57 us; the launch traced here: 56.6 us
  Pallas kernels  54.7 us (96%)
  local copies, waits for them, and re-layouts  1.87 us (3%)
    pallas_call x1, Pallas kernels, body(): pl.pallas_call(kernel, out_shape=jax.ShapeDtypeStruct((TOK, CH), BF16), i...  54.7 us
    unnamed x1, local copies, waits for them, and re-layouts  1.87 us

profile of v4, /device:TPU:4, one launch (start us, length us, event | category | flops | bytes accessed | tf_op | source)
XLA Modules:
  0.0 56.6 jit_solution(14231424859114649852)
XLA Ops:
  0.0 54.7 %ssm_layer.1 = bf16[256,1024]{1,0:T(8,128)(2,1)} custom-call(bf16[256,1024]{1,0:T(8,128)(2,1)} %x_hbm.1, bf16[256,1024]{1,0:T(8,128)(2,1)} %z_hbm.1, bf16[256,128]{1,0:T(8,128)(2,1)} %b_ref.1, bf16[256,128]{1,0:T(8,128)(2,1)} %c_ref.1, f32[16,256]{1,0:T(8,128)} %bitcast.4, f32[16,256]{1,0:T(8,128)} %bitcast.5, bf16[4,1024]{1,0:T(4,128)(2,1)} %kx_ref.1, ...), custom_call_target="tpu_custom_call" | custom-call | tf_op jit(solution)/shard_map/ssm_layer/pallas_call | solution.py:461
  54.7 1.9 %copy.14 = bf16[256,1024]{1,0:T(8,128)(2,1)} copy(bf16[256,1024]{1,0:T(8,128)(2,1)} %ssm_layer.1) | data formatting | bytes 1048576
